TPU v7x, 32 devices: a whole 2x2x4 slice. The times are simulated.
32 devices in a mesh: grp: 2 (over y), slab: 2 (over x), lat: 8 (over z, core).
Axes of the slice: x: 2, y: 2, z: 4, core: 2. Of those that a mesh axis runs over, the one named last changes fastest.
Arguments:
- cond_lists: int32 [64, 16], P(('slab', 'lat')), may hold values from 0 to 31, all different within a row
- regress: float32 [64, 128, 2048], P(('slab', 'lat')), may hold values from -0.09375 to 0.09375
- chol: float32 [64, 128, 128], P(('slab', 'lat')), as said below
- noise: float32 [128, 256, 128], P(('grp', 'slab', 'lat')), parts along dimension 0, may hold values from -6 to 6
- start_field: float32 [64, 256, 128], P(('grp', 'lat')), parts along dimension 0, may hold values from -6 to 6
Outputs:
- field: float32 [128, 256, 128], P(('grp', 'slab', 'lat')), parts along dimension 0
There are 2 independent parts, one for each index of `grp`. A program takes and returns all parts, laid end to end along the dimension named above; an argument that names none is the same for every part. Nothing has to cross between parts.
Inputs may be any that keep to these rules, and one draw needn't show every extreme that they name: `cond_lists`: each row names 16 distinct positions of the previous slab. `chol`: each factor is lower triangular with diagonal entries from 0.3 to 0.7.
All inputs are finite; a program needn't handle non-finite values.
Results may differ from a plain program's by a relative error of at most 0.0001.
Values sent between devices are 32-bit elements; how exact they have to be, the bound alone decides.
No kernel may reach another device: no remote copies, remote signals or barrier semaphores. Data moves between devices by JAX's collectives and lax.ppermute only.
A program may use at most 64 MiB of HBM per device.

v0:
```python
import jax
import jax.numpy as jnp
from jax import lax
from jax.sharding import PartitionSpec as P

PANEL = 64


def passed_along(array, axis, by):
    length = lax.axis_size(axis)
    pairs = [(i, i + by) for i in range(length) if 0 <= i + by < length]
    return lax.ppermute(array, axis, pairs)


def shards(cond_lists, regress, chol, noise, start_field):
    blocks, nreal_here, block_size = noise.shape
    list_length = cond_lists.shape[1]
    front_width = PANEL
    fronts = nreal_here // front_width
    n_slab = lax.axis_size("slab")
    slab_pos = lax.axis_index("slab")
    sections = n_slab + fronts - 1
    factors = regress.reshape(blocks, block_size, list_length, block_size)

    def compute(front_start, previous):
        picked = previous[cond_lists]
        shocks = lax.dynamic_slice_in_dim(noise, front_start, front_width, 1)
        mean_part = jnp.einsum("jakb,jkwb->jwa", factors, picked, precision=lax.Precision.HIGHEST)
        shock_part = jnp.einsum("jab,jwb->jwa", chol, shocks, precision=lax.Precision.HIGHEST)
        return mean_part + shock_part

    def skip(front_start, previous):
        return jnp.zeros((blocks, front_width, block_size), jnp.float32)

    start_box = jnp.zeros((blocks, front_width, block_size), jnp.float32)

    def section(section_step, carry):
        incoming, field_out = carry
        front_index = section_step - slab_pos
        active = (front_index >= 0) & (front_index < fronts)
        front_start = jnp.clip(front_index, 0, fronts - 1) * front_width
        boundary = lax.dynamic_slice_in_dim(start_field, front_start, front_width, 1)
        source = jnp.where(slab_pos == 0, boundary, incoming)
        previous = lax.all_gather(source, "lat", axis=0, tiled=True)
        fresh_blocks = lax.cond(active, compute, skip, front_start, previous)
        old_blocks = lax.dynamic_slice_in_dim(field_out, front_start, front_width, 1)
        kept = jnp.where(active, fresh_blocks, old_blocks)
        field_out = lax.dynamic_update_slice_in_dim(field_out, kept, front_start, 1)
        incoming = passed_along(fresh_blocks, "slab", 1)
        return (incoming, field_out)

    start_out = jnp.zeros((blocks, nreal_here, block_size), jnp.float32)
    incoming, field_out = lax.fori_loop(0, sections, section, (start_box, start_out))
    return field_out


def solution(mesh):
    in_specs = (
        P(("slab", "lat"), None),
        P(("slab", "lat"), None, None),
        P(("slab", "lat"), None, None),
        P(("grp", "slab", "lat"), None, None),
        P(("grp", "lat"), None, None),
    )
    out_specs = P(("grp", "slab", "lat"), None, None)
    return jax.shard_map(shards, mesh=mesh, in_specs=in_specs, out_specs=out_specs, check_vma=False)
```

profile of v0, /device:TPU:0, one launch (start us, length us, event | category | flops | bytes accessed | tf_op | source)
XLA Modules:
  0.0 231.9 jit_solution(2512306260924469446)
XLA Ops:
  6.5 5.4 %copy.8 = f32[4,128,2048]{1,2,0:T(8,128)} copy(f32[4,128,2048]{2,1,0:T(8,128)} %param.10) | data formatting | bytes 8388608 | tf_op args[1]
  11.9 5.4 %copy.9 = f32[4,128,16,128]{3,1,2,0:T(8,128)} copy(f32[4,128,16,128]{1,3,2,0:T(8,128)} %bitcast.9) | data formatting | bytes 8388608 | tf_op jit(solution)/shard_map/while | solution.py:53
  17.4 207.3 %while.16 = (s32[]{:T(128)}, f32[4,64,128]{2,1,0:T(8,128)S(1)}, f32[4,256,128]{2,1,0:T(8,128)S(1)}, s32[]{:T(128)}, pred[]{:T(512)}, /*index=5*/f32[4,256,128]{2...) while((s32[]{:T(128)}, f32[4,64,128]{2,1,0:T(8,128)S(1)}, ...), condition=%wide.region_3.4_spmd, body=%wide.region_0.3_spmd.sunk | while | flops 855737536 | bytes 16127929 | solution.py:53
  19.1 25.7 %all-gather.2.cloned.1.call-done = f32[32,64,128]{2,1,0:T(8,128)} async-done(((f32[4,64,128]{2,1,0:T(8,128)}), f32[32,64,128]{2,1,0:T(8,128)}) %all-gather.2.cloned.1.call-update) | async-done | bytes 1048592 | tf_op jit(solution)/shard_map/while/body/eval_jaxpr/all_gather | solution.py:44
  44.8 9.7 %conditional.2 = (f32[4,64,128]{2,1,0:T(8,128)S(1)}) conditional(s32[]{:T(128)} %convert_element_type.9, () %tuple.42, (s32[4,16]{1,0:T(4,128)S(1)}, f32[32,64,128]{2,1,0:T(8,128)}, f32[4,128,16,128]{3,1,2,0:T(8,128)}, s32[]{:T(128)}, f32[4,256,128]{2,1,0:T(8,128)}, /*index=5*/f32[4,128,128]{2,1,0:T(8,128)S(1)}) %tuple.43), branch_computations={%region_1.1_spmd, %region_2.2_spmd} | conditional | flops 855672000 | bytes 11277870 | solution.py:45
  46.8 6.2 %convolution_bitcast_fusion = f32[4,64,128]{2,1,0:T(8,128)S(1)} fusion(f32[4,16,64,128]{3,2,1,0:T(8,128)S(1)} %bitcast.8, f32[4,128,16,128]{3,1,2,0:T(8,128)} %get-tuple-element.210), kind=kOutput, calls=%fused_computation.2 | convolution fusion | flops 805306368 | bytes 6422528 | tf_op jit(solution)/shard_map/while/body/eval_jaxpr/cond/branch_1_fun/jakb,jkwb->jwa/dot_general | solution.py:28
  55.8 3.4 %collective-permute-done = f32[4,64,128]{2,1,0:T(8,128)S(1)} collective-permute-done((f32[4,64,128]{2,1,0:T(8,128)S(1)}, f32[4,64,128]{2,1,0:T(8,128)S(1)}, u32[]{:S(2)}, u32[]{:S(2)}) %collective-permute-start) | collective-permute-done | bytes 131104 | tf_op jit(solution)/shard_map/while/body/eval_jaxpr/ppermute | solution.py:12
  60.8 23.6 %all-gather.2.cloned.1.call-done = f32[32,64,128]{2,1,0:T(8,128)} async-done(((f32[4,64,128]{2,1,0:T(8,128)}), f32[32,64,128]{2,1,0:T(8,128)}) %all-gather.2.cloned.1.call-update) | async-done | bytes 1048592 | tf_op jit(solution)/shard_map/while/body/eval_jaxpr/all_gather | solution.py:44
  84.4 9.7 %conditional.2 = (f32[4,64,128]{2,1,0:T(8,128)S(1)}) conditional(s32[]{:T(128)} %convert_element_type.9, () %tuple.42, (s32[4,16]{1,0:T(4,128)S(1)}, f32[32,64,128]{2,1,0:T(8,128)}, f32[4,128,16,128]{3,1,2,0:T(8,128)}, s32[]{:T(128)}, f32[4,256,128]{2,1,0:T(8,128)}, /*index=5*/f32[4,128,128]{2,1,0:T(8,128)S(1)}) %tuple.43), branch_computations={%region_1.1_spmd, %region_2.2_spmd} | conditional | flops 855672000 | bytes 11277870 | solution.py:45
  86.4 6.2 %convolution_bitcast_fusion = f32[4,64,128]{2,1,0:T(8,128)S(1)} fusion(f32[4,16,64,128]{3,2,1,0:T(8,128)S(1)} %bitcast.8, f32[4,128,16,128]{3,1,2,0:T(8,128)} %get-tuple-element.210), kind=kOutput, calls=%fused_computation.2 | convolution fusion | flops 805306368 | bytes 6422528 | tf_op jit(solution)/shard_map/while/body/eval_jaxpr/cond/branch_1_fun/jakb,jkwb->jwa/dot_general | solution.py:28
  94.2 3.4 %collective-permute-start = (f32[4,64,128]{2,1,0:T(8,128)S(1)}, f32[4,64,128]{2,1,0:T(8,128)S(1)}, u32[]{:S(2)}, u32[]{:S(2)}) collective-permute-start(f32[4,64,128]{2,1,0:T(8,128)S(1)} %get-tuple-element.376), channel_id=1, source_target_pairs={{0,8},{1,9},{2,10},{3,11},{4,12},{5,13},{6,14},{7,15},{16,24},{17,... | collective-permute-start | bytes 393224 | tf_op jit(solution)/shard_map/while/body/eval_jaxpr/ppermute | solution.py:12
  97.6 3.1 %collective-permute-done = f32[4,64,128]{2,1,0:T(8,128)S(1)} collective-permute-done((f32[4,64,128]{2,1,0:T(8,128)S(1)}, f32[4,64,128]{2,1,0:T(8,128)S(1)}, u32[]{:S(2)}, u32[]{:S(2)}) %collective-permute-start) | collective-permute-done | bytes 131104 | tf_op jit(solution)/shard_map/while/body/eval_jaxpr/ppermute | solution.py:12
  102.3 23.7 %all-gather.2.cloned.1.call-done = f32[32,64,128]{2,1,0:T(8,128)} async-done(((f32[4,64,128]{2,1,0:T(8,128)}), f32[32,64,128]{2,1,0:T(8,128)}) %all-gather.2.cloned.1.call-update) | async-done | bytes 1048592 | tf_op jit(solution)/shard_map/while/body/eval_jaxpr/all_gather | solution.py:44
  126.0 9.7 %conditional.2 = (f32[4,64,128]{2,1,0:T(8,128)S(1)}) conditional(s32[]{:T(128)} %convert_element_type.9, () %tuple.42, (s32[4,16]{1,0:T(4,128)S(1)}, f32[32,64,128]{2,1,0:T(8,128)}, f32[4,128,16,128]{3,1,2,0:T(8,128)}, s32[]{:T(128)}, f32[4,256,128]{2,1,0:T(8,128)}, /*index=5*/f32[4,128,128]{2,1,0:T(8,128)S(1)}) %tuple.43), branch_computations={%region_1.1_spmd, %region_2.2_spmd} | conditional | flops 855672000 | bytes 11277870 | solution.py:45
  128.0 6.2 %convolution_bitcast_fusion = f32[4,64,128]{2,1,0:T(8,128)S(1)} fusion(f32[4,16,64,128]{3,2,1,0:T(8,128)S(1)} %bitcast.8, f32[4,128,16,128]{3,1,2,0:T(8,128)} %get-tuple-element.210), kind=kOutput, calls=%fused_computation.2 | convolution fusion | flops 805306368 | bytes 6422528 | tf_op jit(solution)/shard_map/while/body/eval_jaxpr/cond/branch_1_fun/jakb,jkwb->jwa/dot_general | solution.py:28
  135.7 3.4 %collective-permute-start = (f32[4,64,128]{2,1,0:T(8,128)S(1)}, f32[4,64,128]{2,1,0:T(8,128)S(1)}, u32[]{:S(2)}, u32[]{:S(2)}) collective-permute-start(f32[4,64,128]{2,1,0:T(8,128)S(1)} %get-tuple-element.376), channel_id=1, source_target_pairs={{0,8},{1,9},{2,10},{3,11},{4,12},{5,13},{6,14},{7,15},{16,24},{17,... | collective-permute-start | bytes 393224 | tf_op jit(solution)/shard_map/while/body/eval_jaxpr/ppermute | solution.py:12
  139.1 3.1 %collective-permute-done = f32[4,64,128]{2,1,0:T(8,128)S(1)} collective-permute-done((f32[4,64,128]{2,1,0:T(8,128)S(1)}, f32[4,64,128]{2,1,0:T(8,128)S(1)}, u32[]{:S(2)}, u32[]{:S(2)}) %collective-permute-start) | collective-permute-done | bytes 131104 | tf_op jit(solution)/shard_map/while/body/eval_jaxpr/ppermute | solution.py:12
  143.8 23.4 %all-gather.2.cloned.1.call-done = f32[32,64,128]{2,1,0:T(8,128)} async-done(((f32[4,64,128]{2,1,0:T(8,128)}), f32[32,64,128]{2,1,0:T(8,128)}) %all-gather.2.cloned.1.call-update) | async-done | bytes 1048592 | tf_op jit(solution)/shard_map/while/body/eval_jaxpr/all_gather | solution.py:44
  167.2 9.7 %conditional.2 = (f32[4,64,128]{2,1,0:T(8,128)S(1)}) conditional(s32[]{:T(128)} %convert_element_type.9, () %tuple.42, (s32[4,16]{1,0:T(4,128)S(1)}, f32[32,64,128]{2,1,0:T(8,128)}, f32[4,128,16,128]{3,1,2,0:T(8,128)}, s32[]{:T(128)}, f32[4,256,128]{2,1,0:T(8,128)}, /*index=5*/f32[4,128,128]{2,1,0:T(8,128)S(1)}) %tuple.43), branch_computations={%region_1.1_spmd, %region_2.2_spmd} | conditional | flops 855672000 | bytes 11277870 | solution.py:45
  169.2 6.2 %convolution_bitcast_fusion = f32[4,64,128]{2,1,0:T(8,128)S(1)} fusion(f32[4,16,64,128]{3,2,1,0:T(8,128)S(1)} %bitcast.8, f32[4,128,16,128]{3,1,2,0:T(8,128)} %get-tuple-element.210), kind=kOutput, calls=%fused_computation.2 | convolution fusion | flops 805306368 | bytes 6422528 | tf_op jit(solution)/shard_map/while/body/eval_jaxpr/cond/branch_1_fun/jakb,jkwb->jwa/dot_general | solution.py:28
  176.9 3.4 %collective-permute-start = (f32[4,64,128]{2,1,0:T(8,128)S(1)}, f32[4,64,128]{2,1,0:T(8,128)S(1)}, u32[]{:S(2)}, u32[]{:S(2)}) collective-permute-start(f32[4,64,128]{2,1,0:T(8,128)S(1)} %get-tuple-element.376), channel_id=1, source_target_pairs={{0,8},{1,9},{2,10},{3,11},{4,12},{5,13},{6,14},{7,15},{16,24},{17,... | collective-permute-start | bytes 393224 | tf_op jit(solution)/shard_map/while/body/eval_jaxpr/ppermute | solution.py:12
  185.0 23.4 %all-gather.2.cloned.1.call-done = f32[32,64,128]{2,1,0:T(8,128)} async-done(((f32[4,64,128]{2,1,0:T(8,128)}), f32[32,64,128]{2,1,0:T(8,128)}) %all-gather.2.cloned.1.call-update) | async-done | bytes 1048592 | tf_op jit(solution)/shard_map/while/body/eval_jaxpr/all_gather | solution.py:44
  208.4 13.1 %collective-permute-start = (f32[4,64,128]{2,1,0:T(8,128)S(1)}, f32[4,64,128]{2,1,0:T(8,128)S(1)}, u32[]{:S(2)}, u32[]{:S(2)}) collective-permute-start(f32[4,64,128]{2,1,0:T(8,128)S(1)} %get-tuple-element.376), channel_id=1, source_target_pairs={{0,8},{1,9},{2,10},{3,11},{4,12},{5,13},{6,14},{7,15},{16,24},{17,... | collective-permute-start | bytes 393224 | tf_op jit(solution)/shard_map/while/body/eval_jaxpr/ppermute | solution.py:12
  221.5 3.1 %collective-permute-done = f32[4,64,128]{2,1,0:T(8,128)S(1)} collective-permute-done((f32[4,64,128]{2,1,0:T(8,128)S(1)}, f32[4,64,128]{2,1,0:T(8,128)S(1)}, u32[]{:S(2)}, u32[]{:S(2)}) %collective-permute-start) | collective-permute-done | bytes 131104 | tf_op jit(solution)/shard_map/while/body/eval_jaxpr/ppermute | solution.py:12
  (52 shorter events, 27.5 us)
Async XLA Ops:
  11.9 5.4 %copy-start = (f32[4,128,128]{2,1,0:T(8,128)S(1)}, f32[4,128,128]{2,1,0:T(8,128)}, u32[]{:S(2)}) copy-start(f32[4,128,128]{2,1,0:T(8,128)} %param.11) | copy-start | bytes 786436
  11.9 5.5 %copy-start.2 = (s32[4,16]{1,0:T(4,128)S(1)}, s32[4,16]{1,0:T(4,128)}, u32[]{:S(2)}) copy-start(s32[4,16]{1,0:T(4,128)} %param.9) | copy-start | bytes 772
  17.4 27.4 %all-gather.2.cloned.1.call-start = ((), (), s32[]{:S(2)}) async-start(), calls=%async_computation | async-start | bytes 1179648 | tf_op jit(solution)/shard_map/while/body/eval_jaxpr/all_gather | solution.py:44
  54.5 4.7 %collective-permute-start = (f32[4,64,128]{2,1,0:T(8,128)S(1)}, f32[4,64,128]{2,1,0:T(8,128)S(1)}, u32[]{:S(2)}, u32[]{:S(2)}) collective-permute-start(f32[4,64,128]{2,1,0:T(8,128)S(1)} %get-tuple-element.376), channel_id=1, source_target_pairs={{0,8},{1,9},{2,10},{3,11},{4,12},{5,13},{6,14},{7,15},{16,24},{17,... | collective-permute-start | bytes 393224 | tf_op jit(solution)/shard_map/while/body/eval_jaxpr/ppermute | solution.py:12
  59.2 25.2 %all-gather.2.cloned.1.call-start = ((), (), s32[]{:S(2)}) async-start(), calls=%async_computation | async-start | bytes 1179648 | tf_op jit(solution)/shard_map/while/body/eval_jaxpr/all_gather | solution.py:44
  94.2 6.5 %collective-permute-start = (f32[4,64,128]{2,1,0:T(8,128)S(1)}, f32[4,64,128]{2,1,0:T(8,128)S(1)}, u32[]{:S(2)}, u32[]{:S(2)}) collective-permute-start(f32[4,64,128]{2,1,0:T(8,128)S(1)} %get-tuple-element.376), channel_id=1, source_target_pairs={{0,8},{1,9},{2,10},{3,11},{4,12},{5,13},{6,14},{7,15},{16,24},{17,... | collective-permute-start | bytes 393224 | tf_op jit(solution)/shard_map/while/body/eval_jaxpr/ppermute | solution.py:12
  100.7 25.3 %all-gather.2.cloned.1.call-start = ((), (), s32[]{:S(2)}) async-start(), calls=%async_computation | async-start | bytes 1179648 | tf_op jit(solution)/shard_map/while/body/eval_jaxpr/all_gather | solution.py:44
  135.7 6.5 %collective-permute-start = (f32[4,64,128]{2,1,0:T(8,128)S(1)}, f32[4,64,128]{2,1,0:T(8,128)S(1)}, u32[]{:S(2)}, u32[]{:S(2)}) collective-permute-start(f32[4,64,128]{2,1,0:T(8,128)S(1)} %get-tuple-element.376), channel_id=1, source_target_pairs={{0,8},{1,9},{2,10},{3,11},{4,12},{5,13},{6,14},{7,15},{16,24},{17,... | collective-permute-start | bytes 393224 | tf_op jit(solution)/shard_map/while/body/eval_jaxpr/ppermute | solution.py:12
  142.2 25.0 %all-gather.2.cloned.1.call-start = ((), (), s32[]{:S(2)}) async-start(), calls=%async_computation | async-start | bytes 1179648 | tf_op jit(solution)/shard_map/while/body/eval_jaxpr/all_gather | solution.py:44
  176.9 6.5 %collective-permute-start = (f32[4,64,128]{2,1,0:T(8,128)S(1)}, f32[4,64,128]{2,1,0:T(8,128)S(1)}, u32[]{:S(2)}, u32[]{:S(2)}) collective-permute-start(f32[4,64,128]{2,1,0:T(8,128)S(1)} %get-tuple-element.376), channel_id=1, source_target_pairs={{0,8},{1,9},{2,10},{3,11},{4,12},{5,13},{6,14},{7,15},{16,24},{17,... | collective-permute-start | bytes 393224 | tf_op jit(solution)/shard_map/while/body/eval_jaxpr/ppermute | solution.py:12
  183.4 25.0 %all-gather.2.cloned.1.call-start = ((), (), s32[]{:S(2)}) async-start(), calls=%async_computation | async-start | bytes 1179648 | tf_op jit(solution)/shard_map/while/body/eval_jaxpr/all_gather | solution.py:44
  208.4 16.2 %collective-permute-start = (f32[4,64,128]{2,1,0:T(8,128)S(1)}, f32[4,64,128]{2,1,0:T(8,128)S(1)}, u32[]{:S(2)}, u32[]{:S(2)}) collective-permute-start(f32[4,64,128]{2,1,0:T(8,128)S(1)} %get-tuple-element.376), channel_id=1, source_target_pairs={{0,8},{1,9},{2,10},{3,11},{4,12},{5,13},{6,14},{7,15},{16,24},{17,... | collective-permute-start | bytes 393224 | tf_op jit(solution)/shard_map/while/body/eval_jaxpr/ppermute | solution.py:12
  224.6 0.8 copy-start.1
Sparse Core Ops, SparseCore 0:
  19.8 24.9 all-gather.1
  61.6 22.7 all-gather.1
  103.1 22.8 all-gather.1
  144.3 22.8 all-gather.1
  185.5 22.8 all-gather.1
where the time goes:
time: 233 us; the launch traced here: 232 us
  waiting for transfers between devices  136 us (58%)
  matrix products  30.8 us (13%)
  starting transfers between devices  24.6 us (11%)
  local copies, waits for them, and re-layouts  19.6 us (8%)
  between operations  13.1 us (6%)
  other arithmetic  8.07 us (3%)
    all_gather x5, waiting for transfers between devices, section(): previous = lax.all_gather(source, 'lat', axis=0, tiled=True)  120 us
    dot_general x4, matrix products, compute(): jnp.einsum('jakb,jkwb->jwa', factors, picked, precision=lax.Precision.HIG...  24.7 us
    ppermute x5, starting transfers between devices, passed_along(): return lax.ppermute(array, axis, pairs)  24.5 us
    ppermute x5, waiting for transfers between devices, passed_along(): return lax.ppermute(array, axis, pairs)  15.7 us
    select_n x5, other arithmetic, section(): source = jnp.where(slab_pos == 0, boundary, incoming)  7.89 us
    gather x4, local copies, waits for them, and re-layouts, compute(): picked = previous[cond_lists]  7.62 us
    unnamed x7, local copies, waits for them, and re-layouts  6.15 us
    dot_general x4, matrix products, compute(): jnp.einsum('jab,jwb->jwa', chol, shocks, precision=lax.Precision.HIGHEST)  6.13 us
  transfers between devices with their start and end apart: 10, of which 10 were waited for; matrix products, arithmetic and copies ran while one was open for 0% of the time, Pallas kernels for 0%

commit v1 on v0

--- a/solution.py
+++ b/solution.py
@@ -41,7 +41,24 @@
         front_start = jnp.clip(front_index, 0, fronts - 1) * front_width
         boundary = lax.dynamic_slice_in_dim(start_field, front_start, front_width, 1)
         source = jnp.where(slab_pos == 0, boundary, incoming)
-        previous = lax.all_gather(source, "lat", axis=0, tiled=True)
+        ways, here, step = (lax.axis_size("lat"), lax.axis_index("lat"), source.shape[0])
+        shape = [n * ways if d == 0 else n for d, n in enumerate(source.shape)]
+        previous = lax.dynamic_update_slice_in_dim(
+            jnp.zeros(shape, source.dtype), source, here * step, axis=0
+        )
+        going_up = going_down = source
+        for far in range(1, ways // 2 + 1):
+            going_up = lax.ppermute(going_up, "lat", [(d, (d + 1) % ways) for d in range(ways)])
+            previous = lax.dynamic_update_slice_in_dim(
+                previous, going_up, (here - far) % ways * step, axis=0
+            )
+            if 2 * far < ways:
+                going_down = lax.ppermute(
+                    going_down, "lat", [(d, (d - 1) % ways) for d in range(ways)]
+                )
+                previous = lax.dynamic_update_slice_in_dim(
+                    previous, going_down, (here + far) % ways * step, axis=0
+                )
         fresh_blocks = lax.cond(active, compute, skip, front_start, previous)
         old_blocks = lax.dynamic_slice_in_dim(field_out, front_start, front_width, 1)
         kept = jnp.where(active, fresh_blocks, old_blocks)

time: 233 us -> 220 us (0.944)
  waiting for transfers between devices: 136 us -> 76.8 us
  starting transfers between devices: 24.6 us -> 82.3 us
  between operations: 13.1 us -> 0.02 us
  other arithmetic: 8.07 us -> 12.6 us
  local copies, waits for them, and re-layouts: 19.6 us -> 15.6 us
    all_gather x5 -> x0, waiting for transfers between devices: 120 us -> none  [section(): previous = lax.all_gather(source, 'lat', axis=0, tiled=True)]
    ppermute x0 -> x35, waiting for transfers between devices: none -> 72.2 us  [the longest x20 72.1 us: section(): lax.ppermute(going_up, 'lat', [(d, (d + 1) % ways) for d in range(ways)])]
    ppermute x0 -> x35, starting transfers between devices: none -> 54.7 us  [the longest x15 53.9 us: section(): lax.ppermute(going_down, 'lat', [(d, (d - 1) % ways) for d in range(ways)])]
    ppermute x5, waiting for transfers between devices: 15.7 us -> 4.55 us  [passed_along(): return lax.ppermute(array, axis, pairs)]
    dynamic_update_slice x5, other arithmetic: 0.14 us -> 7.93 us  [section(): field_out = lax.dynamic_update_slice_in_dim(field_out, kept, front_start, 1)]
    gather x4, local copies, waits for them, and re-layouts: 7.62 us -> 2.74 us  [compute(): picked = previous[cond_lists]]
    select_n x5, other arithmetic: 7.89 us -> 4.62 us  [section(): source = jnp.where(slab_pos == 0, boundary, incoming)]
    ppermute x5, starting transfers between devices: 24.5 us -> 27.7 us  [passed_along(): return lax.ppermute(array, axis, pairs)]
  transfers between devices with their start and end apart: 10 -> 40, of which waited for: 10 -> 26; matrix products, arithmetic and copies ran while one was open for 0% -> 4% of each run, Pallas kernels for 0% -> 0%
where the time goes in v1:
time: 220 us; the launch traced here: 219 us
  starting transfers between devices  82.3 us (37%)
  waiting for transfers between devices  76.8 us (35%)
  matrix products  30.8 us (14%)
  local copies, waits for them, and re-layouts  15.6 us (7%)
  other arithmetic  12.6 us (6%)
    ppermute x20, waiting for transfers between devices, section(): lax.ppermute(going_up, 'lat', [(d, (d + 1) % ways) for d in range(ways)])  72.1 us
    ppermute x15, starting transfers between devices, section(): lax.ppermute(going_down, 'lat', [(d, (d - 1) % ways) for d in range(ways)])  53.9 us
    ppermute x5, starting transfers between devices, passed_along(): return lax.ppermute(array, axis, pairs)  27.7 us
    dot_general x4, matrix products, compute(): jnp.einsum('jakb,jkwb->jwa', factors, picked, precision=lax.Precision.HIG...  24.7 us
    dynamic_update_slice x5, other arithmetic, section(): field_out = lax.dynamic_update_slice_in_dim(field_out, kept, front_start, 1)  7.93 us
    dot_general x4, matrix products, compute(): jnp.einsum('jab,jwb->jwa', chol, shocks, precision=lax.Precision.HIGHEST)  6.12 us
    while x1, local copies, waits for them, and re-layouts, shards(): lax.fori_loop(0, sections, section, (start_box, start_out))  5.42 us
    unnamed x5, local copies, waits for them, and re-layouts  5.38 us
  transfers between devices with their start and end apart: 40, of which 26 were waited for; matrix products, arithmetic and copies ran while one was open for 4% of the time, Pallas kernels for 0%

profile of v1, /device:TPU:0, one launch (start us, length us, event | category | flops | bytes accessed | tf_op | source)
XLA Modules:
  0.0 219.2 jit_solution(1182586097820858156)
XLA Ops:
  0.0 5.4 %copy.6 = f32[4,128,2048]{1,2,0:T(8,128)} copy(f32[4,128,2048]{2,1,0:T(8,128)} %param.10) | data formatting | bytes 8388608 | tf_op args[1]
  5.4 5.4 %copy.7 = f32[4,128,16,128]{3,1,2,0:T(8,128)} copy(f32[4,128,16,128]{1,3,2,0:T(8,128)} %bitcast.11) | data formatting | bytes 8388608 | tf_op jit(solution)/shard_map/while | solution.py:70
  11.7 207.6 %while.17 = (s32[]{:T(128)}, f32[4,64,128]{2,1,0:T(8,128)S(1)}, f32[4,256,128]{2,1,0:T(8,128)}, s32[]{:T(128)}, pred[]{:T(512)}, /*index=5*/f32[4,256,128]{2,1,0...) while((s32[]{:T(128)}, f32[4,64,128]{2,1,0:T(8,128)S(1)}, ...), condition=%wide.region_3.4_spmd, body=%wide.region_0.3_spmd.sunk | while | flops 855737664 | bytes 19406392 | solution.py:70
  13.2 4.1 %collective-permute-start.1 = (f32[4,64,128]{2,1,0:T(8,128)S(1)}, f32[4,64,128]{2,1,0:T(8,128)S(1)}, u32[]{:S(2)}, u32[]{:S(2)}) collective-permute-start(f32[4,64,128]{2,1,0:T(8,128)S(1)} %dynamic-slice_select_fusion.2), channel_id=1, source_target_pairs={{0,7},{1,0},{2,1},{3,2},{4,3},{5,4},{6,5},{7,6},{8,15},{9,8},{10,9... | collective-permute-start | bytes 393224 | tf_op jit(solution)/shard_map/while/body/eval_jaxpr/ppermute | solution.py:56
  26.9 3.7 %collective-permute-start.5 = (f32[4,64,128]{2,1,0:T(8,128)S(1)}, f32[4,64,128]{2,1,0:T(8,128)S(1)}, u32[]{:S(2)}, u32[]{:S(2)}) collective-permute-start(f32[4,64,128]{2,1,0:T(8,128)S(1)} %collective-permute-done.3), channel_id=1, source_target_pairs={{0,7},{1,0},{2,1},{3,2},{4,3},{5,4},{6,5},{7,6},{8,15},{9,8},{10,9... | collective-permute-start | bytes 393224 | tf_op jit(solution)/shard_map/while/body/eval_jaxpr/ppermute | solution.py:56
  33.3 6.2 %collective-permute-done.6 = f32[4,64,128]{2,1,0:T(8,128)S(1)} collective-permute-done((f32[4,64,128]{2,1,0:T(8,128)S(1)}, f32[4,64,128]{2,1,0:T(8,128)S(1)}, u32[]{:S(2)}, u32[]{:S(2)}) %collective-permute-start.6) | collective-permute-done | bytes 131104 | tf_op jit(solution)/shard_map/while/body/eval_jaxpr/ppermute | solution.py:51
  39.5 8.9 %conditional.2 = (f32[4,64,128]{2,1,0:T(8,128)S(1)}) conditional(s32[]{:T(128)} %convert_element_type.11, () %tuple.137, (s32[]{:T(128)}, f32[4,64,128]{2,1,0:T(8,128)S(1)}, s32[]{:T(128)}, f32[4,64,128]{2,1,0:T(8,128)S(1)}, s32[]{:T(128)}, /*index=5*/s32[]{:T(128)}, f32[4,64,128]{2,1,0:T(8,128)S(1)}, s32[]{:T(128)}, ...), branch_computations={%region_1.1_spmd, %region_2.2_spmd.clone.clone} | conditional | flops 855672128 | bytes 14424849 | solution.py:62
  40.7 6.2 %convolution_bitcast_fusion = f32[4,64,128]{2,1,0:T(8,128)S(1)} fusion(f32[4,16,64,128]{3,2,1,0:T(8,128)S(1)} %bitcast.10, f32[4,128,16,128]{3,1,2,0:T(8,128)} %get-tuple-element.985), kind=kOutput, calls=%fused_computation.2 | convolution fusion | flops 805306368 | bytes 6422528 | tf_op jit(solution)/shard_map/while/body/eval_jaxpr/cond/branch_1_fun/jakb,jkwb->jwa/dot_general | solution.py:28
  59.5 3.6 %collective-permute-start.3 = (f32[4,64,128]{2,1,0:T(8,128)S(1)}, f32[4,64,128]{2,1,0:T(8,128)S(1)}, u32[]{:S(2)}, u32[]{:S(2)}) collective-permute-start(f32[4,64,128]{2,1,0:T(8,128)S(1)} %collective-permute-done.1), channel_id=1, source_target_pairs={{0,7},{1,0},{2,1},{3,2},{4,3},{5,4},{6,5},{7,6},{8,15},{9,8},{10,9... | collective-permute-start | bytes 393224 | tf_op jit(solution)/shard_map/while/body/eval_jaxpr/ppermute | solution.py:56
  65.8 3.6 %collective-permute-start.5 = (f32[4,64,128]{2,1,0:T(8,128)S(1)}, f32[4,64,128]{2,1,0:T(8,128)S(1)}, u32[]{:S(2)}, u32[]{:S(2)}) collective-permute-start(f32[4,64,128]{2,1,0:T(8,128)S(1)} %collective-permute-done.3), channel_id=1, source_target_pairs={{0,7},{1,0},{2,1},{3,2},{4,3},{5,4},{6,5},{7,6},{8,15},{9,8},{10,9... | collective-permute-start | bytes 393224 | tf_op jit(solution)/shard_map/while/body/eval_jaxpr/ppermute | solution.py:56
  72.0 6.2 %collective-permute-done.6 = f32[4,64,128]{2,1,0:T(8,128)S(1)} collective-permute-done((f32[4,64,128]{2,1,0:T(8,128)S(1)}, f32[4,64,128]{2,1,0:T(8,128)S(1)}, u32[]{:S(2)}, u32[]{:S(2)}) %collective-permute-start.6) | collective-permute-done | bytes 131104 | tf_op jit(solution)/shard_map/while/body/eval_jaxpr/ppermute | solution.py:51
  78.2 8.9 %conditional.2 = (f32[4,64,128]{2,1,0:T(8,128)S(1)}) conditional(s32[]{:T(128)} %convert_element_type.11, () %tuple.137, (s32[]{:T(128)}, f32[4,64,128]{2,1,0:T(8,128)S(1)}, s32[]{:T(128)}, f32[4,64,128]{2,1,0:T(8,128)S(1)}, s32[]{:T(128)}, /*index=5*/s32[]{:T(128)}, f32[4,64,128]{2,1,0:T(8,128)S(1)}, s32[]{:T(128)}, ...), branch_computations={%region_1.1_spmd, %region_2.2_spmd.clone.clone} | conditional | flops 855672128 | bytes 14424849 | solution.py:62
  79.4 6.2 %convolution_bitcast_fusion = f32[4,64,128]{2,1,0:T(8,128)S(1)} fusion(f32[4,16,64,128]{3,2,1,0:T(8,128)S(1)} %bitcast.10, f32[4,128,16,128]{3,1,2,0:T(8,128)} %get-tuple-element.985), kind=kOutput, calls=%fused_computation.2 | convolution fusion | flops 805306368 | bytes 6422528 | tf_op jit(solution)/shard_map/while/body/eval_jaxpr/cond/branch_1_fun/jakb,jkwb->jwa/dot_general | solution.py:28
  87.1 4.4 %collective-permute-start.7 = (f32[4,64,128]{2,1,0:T(8,128)S(1)}, f32[4,64,128]{2,1,0:T(8,128)S(1)}, u32[]{:S(2)}, u32[]{:S(2)}) collective-permute-start(f32[4,64,128]{2,1,0:T(8,128)S(1)} %get-tuple-element.1155), channel_id=1, source_target_pairs={{0,8},{1,9},{2,10},{3,11},{4,12},{5,13},{6,14},{7,15},{16,24},{17,... | collective-permute-start | bytes 393224 | tf_op jit(solution)/shard_map/while/body/eval_jaxpr/ppermute | solution.py:12
  113.8 6.2 %collective-permute-done.6 = f32[4,64,128]{2,1,0:T(8,128)S(1)} collective-permute-done((f32[4,64,128]{2,1,0:T(8,128)S(1)}, f32[4,64,128]{2,1,0:T(8,128)S(1)}, u32[]{:S(2)}, u32[]{:S(2)}) %collective-permute-start.6) | collective-permute-done | bytes 131104 | tf_op jit(solution)/shard_map/while/body/eval_jaxpr/ppermute | solution.py:51
  120.0 8.9 %conditional.2 = (f32[4,64,128]{2,1,0:T(8,128)S(1)}) conditional(s32[]{:T(128)} %convert_element_type.11, () %tuple.137, (s32[]{:T(128)}, f32[4,64,128]{2,1,0:T(8,128)S(1)}, s32[]{:T(128)}, f32[4,64,128]{2,1,0:T(8,128)S(1)}, s32[]{:T(128)}, /*index=5*/s32[]{:T(128)}, f32[4,64,128]{2,1,0:T(8,128)S(1)}, s32[]{:T(128)}, ...), branch_computations={%region_1.1_spmd, %region_2.2_spmd.clone.clone} | conditional | flops 855672128 | bytes 14424849 | solution.py:62
  121.2 6.2 %convolution_bitcast_fusion = f32[4,64,128]{2,1,0:T(8,128)S(1)} fusion(f32[4,16,64,128]{3,2,1,0:T(8,128)S(1)} %bitcast.10, f32[4,128,16,128]{3,1,2,0:T(8,128)} %get-tuple-element.985), kind=kOutput, calls=%fused_computation.2 | convolution fusion | flops 805306368 | bytes 6422528 | tf_op jit(solution)/shard_map/while/body/eval_jaxpr/cond/branch_1_fun/jakb,jkwb->jwa/dot_general | solution.py:28
  128.9 4.4 %collective-permute-start.7 = (f32[4,64,128]{2,1,0:T(8,128)S(1)}, f32[4,64,128]{2,1,0:T(8,128)S(1)}, u32[]{:S(2)}, u32[]{:S(2)}) collective-permute-start(f32[4,64,128]{2,1,0:T(8,128)S(1)} %get-tuple-element.1155), channel_id=1, source_target_pairs={{0,8},{1,9},{2,10},{3,11},{4,12},{5,13},{6,14},{7,15},{16,24},{17,... | collective-permute-start | bytes 393224 | tf_op jit(solution)/shard_map/while/body/eval_jaxpr/ppermute | solution.py:12
  155.5 6.2 %collective-permute-done.6 = f32[4,64,128]{2,1,0:T(8,128)S(1)} collective-permute-done((f32[4,64,128]{2,1,0:T(8,128)S(1)}, f32[4,64,128]{2,1,0:T(8,128)S(1)}, u32[]{:S(2)}, u32[]{:S(2)}) %collective-permute-start.6) | collective-permute-done | bytes 131104 | tf_op jit(solution)/shard_map/while/body/eval_jaxpr/ppermute | solution.py:51
  161.7 8.9 %conditional.2 = (f32[4,64,128]{2,1,0:T(8,128)S(1)}) conditional(s32[]{:T(128)} %convert_element_type.11, () %tuple.137, (s32[]{:T(128)}, f32[4,64,128]{2,1,0:T(8,128)S(1)}, s32[]{:T(128)}, f32[4,64,128]{2,1,0:T(8,128)S(1)}, s32[]{:T(128)}, /*index=5*/s32[]{:T(128)}, f32[4,64,128]{2,1,0:T(8,128)S(1)}, s32[]{:T(128)}, ...), branch_computations={%region_1.1_spmd, %region_2.2_spmd.clone.clone} | conditional | flops 855672128 | bytes 14424849 | solution.py:62
  162.9 6.2 %convolution_bitcast_fusion = f32[4,64,128]{2,1,0:T(8,128)S(1)} fusion(f32[4,16,64,128]{3,2,1,0:T(8,128)S(1)} %bitcast.10, f32[4,128,16,128]{3,1,2,0:T(8,128)} %get-tuple-element.985), kind=kOutput, calls=%fused_computation.2 | convolution fusion | flops 805306368 | bytes 6422528 | tf_op jit(solution)/shard_map/while/body/eval_jaxpr/cond/branch_1_fun/jakb,jkwb->jwa/dot_general | solution.py:28
  170.6 4.4 %collective-permute-start.7 = (f32[4,64,128]{2,1,0:T(8,128)S(1)}, f32[4,64,128]{2,1,0:T(8,128)S(1)}, u32[]{:S(2)}, u32[]{:S(2)}) collective-permute-start(f32[4,64,128]{2,1,0:T(8,128)S(1)} %get-tuple-element.1155), channel_id=1, source_target_pairs={{0,8},{1,9},{2,10},{3,11},{4,12},{5,13},{6,14},{7,15},{16,24},{17,... | collective-permute-start | bytes 393224 | tf_op jit(solution)/shard_map/while/body/eval_jaxpr/ppermute | solution.py:12
  197.3 6.2 %collective-permute-done.6 = f32[4,64,128]{2,1,0:T(8,128)S(1)} collective-permute-done((f32[4,64,128]{2,1,0:T(8,128)S(1)}, f32[4,64,128]{2,1,0:T(8,128)S(1)}, u32[]{:S(2)}, u32[]{:S(2)}) %collective-permute-start.6) | collective-permute-done | bytes 131104 | tf_op jit(solution)/shard_map/while/body/eval_jaxpr/ppermute | solution.py:51
  203.5 13.3 %collective-permute-start.7 = (f32[4,64,128]{2,1,0:T(8,128)S(1)}, f32[4,64,128]{2,1,0:T(8,128)S(1)}, u32[]{:S(2)}, u32[]{:S(2)}) collective-permute-start(f32[4,64,128]{2,1,0:T(8,128)S(1)} %get-tuple-element.1155), channel_id=1, source_target_pairs={{0,8},{1,9},{2,10},{3,11},{4,12},{5,13},{6,14},{7,15},{16,24},{17,... | collective-permute-start | bytes 393224 | tf_op jit(solution)/shard_map/while/body/eval_jaxpr/ppermute | solution.py:12
  (141 shorter events, 110.4 us)
Async XLA Ops:
  12.6 7.3 %collective-permute-start = (f32[4,64,128]{2,1,0:T(8,128)S(1)}, f32[4,64,128]{2,1,0:T(8,128)S(1)}, u32[]{:S(2)}, u32[]{:S(2)}) collective-permute-start(f32[4,64,128]{2,1,0:T(8,128)S(1)} %dynamic-slice_select_fusion.2), channel_id=1, source_target_pairs={{0,1},{1,2},{2,3},{3,4},{4,5},{5,6},{6,7},{7,0},{8,9},{9,10},{10,1... | collective-permute-start | bytes 393224 | tf_op jit(solution)/shard_map/while/body/eval_jaxpr/ppermute | solution.py:51
  13.2 6.8 %collective-permute-start.1 = (f32[4,64,128]{2,1,0:T(8,128)S(1)}, f32[4,64,128]{2,1,0:T(8,128)S(1)}, u32[]{:S(2)}, u32[]{:S(2)}) collective-permute-start(f32[4,64,128]{2,1,0:T(8,128)S(1)} %dynamic-slice_select_fusion.2), channel_id=1, source_target_pairs={{0,7},{1,0},{2,1},{3,2},{4,3},{5,4},{6,5},{7,6},{8,15},{9,8},{10,9... | collective-permute-start | bytes 393224 | tf_op jit(solution)/shard_map/while/body/eval_jaxpr/ppermute | solution.py:56
  19.9 6.9 %collective-permute-start.2 = (f32[4,64,128]{2,1,0:T(8,128)S(1)}, f32[4,64,128]{2,1,0:T(8,128)S(1)}, u32[]{:S(2)}, u32[]{:S(2)}) collective-permute-start(f32[4,64,128]{2,1,0:T(8,128)S(1)} %collective-permute-done), channel_id=1, source_target_pairs={{0,1},{1,2},{2,3},{3,4},{4,5},{5,6},{6,7},{7,0},{8,9},{9,10},{10,1... | collective-permute-start | bytes 393224 | tf_op jit(solution)/shard_map/while/body/eval_jaxpr/ppermute | solution.py:51
  19.9 7.0 %collective-permute-start.3 = (f32[4,64,128]{2,1,0:T(8,128)S(1)}, f32[4,64,128]{2,1,0:T(8,128)S(1)}, u32[]{:S(2)}, u32[]{:S(2)}) collective-permute-start(f32[4,64,128]{2,1,0:T(8,128)S(1)} %collective-permute-done.1), channel_id=1, source_target_pairs={{0,7},{1,0},{2,1},{3,2},{4,3},{5,4},{6,5},{7,6},{8,15},{9,8},{10,9... | collective-permute-start | bytes 393224 | tf_op jit(solution)/shard_map/while/body/eval_jaxpr/ppermute | solution.py:56
  26.8 6.5 %collective-permute-start.4 = (f32[4,64,128]{2,1,0:T(8,128)S(1)}, f32[4,64,128]{2,1,0:T(8,128)S(1)}, u32[]{:S(2)}, u32[]{:S(2)}) collective-permute-start(f32[4,64,128]{2,1,0:T(8,128)S(1)} %collective-permute-done.2), channel_id=1, source_target_pairs={{0,1},{1,2},{2,3},{3,4},{4,5},{5,6},{6,7},{7,0},{8,9},{9,10},{10,1... | collective-permute-start | bytes 393224 | tf_op jit(solution)/shard_map/while/body/eval_jaxpr/ppermute | solution.py:51
  26.9 6.4 %collective-permute-start.5 = (f32[4,64,128]{2,1,0:T(8,128)S(1)}, f32[4,64,128]{2,1,0:T(8,128)S(1)}, u32[]{:S(2)}, u32[]{:S(2)}) collective-permute-start(f32[4,64,128]{2,1,0:T(8,128)S(1)} %collective-permute-done.3), channel_id=1, source_target_pairs={{0,7},{1,0},{2,1},{3,2},{4,3},{5,4},{6,5},{7,6},{8,15},{9,8},{10,9... | collective-permute-start | bytes 393224 | tf_op jit(solution)/shard_map/while/body/eval_jaxpr/ppermute | solution.py:56
  53.2 6.3 %collective-permute-start = (f32[4,64,128]{2,1,0:T(8,128)S(1)}, f32[4,64,128]{2,1,0:T(8,128)S(1)}, u32[]{:S(2)}, u32[]{:S(2)}) collective-permute-start(f32[4,64,128]{2,1,0:T(8,128)S(1)} %dynamic-slice_select_fusion.2), channel_id=1, source_target_pairs={{0,1},{1,2},{2,3},{3,4},{4,5},{5,6},{6,7},{7,0},{8,9},{9,10},{10,1... | collective-permute-start | bytes 393224 | tf_op jit(solution)/shard_map/while/body/eval_jaxpr/ppermute | solution.py:51
  53.2 6.3 %collective-permute-start.1 = (f32[4,64,128]{2,1,0:T(8,128)S(1)}, f32[4,64,128]{2,1,0:T(8,128)S(1)}, u32[]{:S(2)}, u32[]{:S(2)}) collective-permute-start(f32[4,64,128]{2,1,0:T(8,128)S(1)} %dynamic-slice_select_fusion.2), channel_id=1, source_target_pairs={{0,7},{1,0},{2,1},{3,2},{4,3},{5,4},{6,5},{7,6},{8,15},{9,8},{10,9... | collective-permute-start | bytes 393224 | tf_op jit(solution)/shard_map/while/body/eval_jaxpr/ppermute | solution.py:56
  59.5 6.3 %collective-permute-start.2 = (f32[4,64,128]{2,1,0:T(8,128)S(1)}, f32[4,64,128]{2,1,0:T(8,128)S(1)}, u32[]{:S(2)}, u32[]{:S(2)}) collective-permute-start(f32[4,64,128]{2,1,0:T(8,128)S(1)} %collective-permute-done), channel_id=1, source_target_pairs={{0,1},{1,2},{2,3},{3,4},{4,5},{5,6},{6,7},{7,0},{8,9},{9,10},{10,1... | collective-permute-start | bytes 393224 | tf_op jit(solution)/shard_map/while/body/eval_jaxpr/ppermute | solution.py:51
  59.5 6.3 %collective-permute-start.3 = (f32[4,64,128]{2,1,0:T(8,128)S(1)}, f32[4,64,128]{2,1,0:T(8,128)S(1)}, u32[]{:S(2)}, u32[]{:S(2)}) collective-permute-start(f32[4,64,128]{2,1,0:T(8,128)S(1)} %collective-permute-done.1), channel_id=1, source_target_pairs={{0,7},{1,0},{2,1},{3,2},{4,3},{5,4},{6,5},{7,6},{8,15},{9,8},{10,9... | collective-permute-start | bytes 393224 | tf_op jit(solution)/shard_map/while/body/eval_jaxpr/ppermute | solution.py:56
  87.1 6.9 %collective-permute-start.7 = (f32[4,64,128]{2,1,0:T(8,128)S(1)}, f32[4,64,128]{2,1,0:T(8,128)S(1)}, u32[]{:S(2)}, u32[]{:S(2)}) collective-permute-start(f32[4,64,128]{2,1,0:T(8,128)S(1)} %get-tuple-element.1155), channel_id=1, source_target_pairs={{0,8},{1,9},{2,10},{3,11},{4,12},{5,13},{6,14},{7,15},{16,24},{17,... | collective-permute-start | bytes 393224 | tf_op jit(solution)/shard_map/while/body/eval_jaxpr/ppermute | solution.py:12
  94.9 6.3 %collective-permute-start = (f32[4,64,128]{2,1,0:T(8,128)S(1)}, f32[4,64,128]{2,1,0:T(8,128)S(1)}, u32[]{:S(2)}, u32[]{:S(2)}) collective-permute-start(f32[4,64,128]{2,1,0:T(8,128)S(1)} %dynamic-slice_select_fusion.2), channel_id=1, source_target_pairs={{0,1},{1,2},{2,3},{3,4},{4,5},{5,6},{6,7},{7,0},{8,9},{9,10},{10,1... | collective-permute-start | bytes 393224 | tf_op jit(solution)/shard_map/while/body/eval_jaxpr/ppermute | solution.py:51
  95.0 6.3 %collective-permute-start.1 = (f32[4,64,128]{2,1,0:T(8,128)S(1)}, f32[4,64,128]{2,1,0:T(8,128)S(1)}, u32[]{:S(2)}, u32[]{:S(2)}) collective-permute-start(f32[4,64,128]{2,1,0:T(8,128)S(1)} %dynamic-slice_select_fusion.2), channel_id=1, source_target_pairs={{0,7},{1,0},{2,1},{3,2},{4,3},{5,4},{6,5},{7,6},{8,15},{9,8},{10,9... | collective-permute-start | bytes 393224 | tf_op jit(solution)/shard_map/while/body/eval_jaxpr/ppermute | solution.py:56
  101.3 6.3 %collective-permute-start.2 = (f32[4,64,128]{2,1,0:T(8,128)S(1)}, f32[4,64,128]{2,1,0:T(8,128)S(1)}, u32[]{:S(2)}, u32[]{:S(2)}) collective-permute-start(f32[4,64,128]{2,1,0:T(8,128)S(1)} %collective-permute-done), channel_id=1, source_target_pairs={{0,1},{1,2},{2,3},{3,4},{4,5},{5,6},{6,7},{7,0},{8,9},{9,10},{10,1... | collective-permute-start | bytes 393224 | tf_op jit(solution)/shard_map/while/body/eval_jaxpr/ppermute | solution.py:51
  101.3 6.3 %collective-permute-start.3 = (f32[4,64,128]{2,1,0:T(8,128)S(1)}, f32[4,64,128]{2,1,0:T(8,128)S(1)}, u32[]{:S(2)}, u32[]{:S(2)}) collective-permute-start(f32[4,64,128]{2,1,0:T(8,128)S(1)} %collective-permute-done.1), channel_id=1, source_target_pairs={{0,7},{1,0},{2,1},{3,2},{4,3},{5,4},{6,5},{7,6},{8,15},{9,8},{10,9... | collective-permute-start | bytes 393224 | tf_op jit(solution)/shard_map/while/body/eval_jaxpr/ppermute | solution.py:56
  128.9 6.9 %collective-permute-start.7 = (f32[4,64,128]{2,1,0:T(8,128)S(1)}, f32[4,64,128]{2,1,0:T(8,128)S(1)}, u32[]{:S(2)}, u32[]{:S(2)}) collective-permute-start(f32[4,64,128]{2,1,0:T(8,128)S(1)} %get-tuple-element.1155), channel_id=1, source_target_pairs={{0,8},{1,9},{2,10},{3,11},{4,12},{5,13},{6,14},{7,15},{16,24},{17,... | collective-permute-start | bytes 393224 | tf_op jit(solution)/shard_map/while/body/eval_jaxpr/ppermute | solution.py:12
  136.7 6.3 %collective-permute-start = (f32[4,64,128]{2,1,0:T(8,128)S(1)}, f32[4,64,128]{2,1,0:T(8,128)S(1)}, u32[]{:S(2)}, u32[]{:S(2)}) collective-permute-start(f32[4,64,128]{2,1,0:T(8,128)S(1)} %dynamic-slice_select_fusion.2), channel_id=1, source_target_pairs={{0,1},{1,2},{2,3},{3,4},{4,5},{5,6},{6,7},{7,0},{8,9},{9,10},{10,1... | collective-permute-start | bytes 393224 | tf_op jit(solution)/shard_map/while/body/eval_jaxpr/ppermute | solution.py:51
  143.0 6.3 %collective-permute-start.2 = (f32[4,64,128]{2,1,0:T(8,128)S(1)}, f32[4,64,128]{2,1,0:T(8,128)S(1)}, u32[]{:S(2)}, u32[]{:S(2)}) collective-permute-start(f32[4,64,128]{2,1,0:T(8,128)S(1)} %collective-permute-done), channel_id=1, source_target_pairs={{0,1},{1,2},{2,3},{3,4},{4,5},{5,6},{6,7},{7,0},{8,9},{9,10},{10,1... | collective-permute-start | bytes 393224 | tf_op jit(solution)/shard_map/while/body/eval_jaxpr/ppermute | solution.py:51
  143.0 6.3 %collective-permute-start.3 = (f32[4,64,128]{2,1,0:T(8,128)S(1)}, f32[4,64,128]{2,1,0:T(8,128)S(1)}, u32[]{:S(2)}, u32[]{:S(2)}) collective-permute-start(f32[4,64,128]{2,1,0:T(8,128)S(1)} %collective-permute-done.1), channel_id=1, source_target_pairs={{0,7},{1,0},{2,1},{3,2},{4,3},{5,4},{6,5},{7,6},{8,15},{9,8},{10,9... | collective-permute-start | bytes 393224 | tf_op jit(solution)/shard_map/while/body/eval_jaxpr/ppermute | solution.py:56
  170.6 6.9 %collective-permute-start.7 = (f32[4,64,128]{2,1,0:T(8,128)S(1)}, f32[4,64,128]{2,1,0:T(8,128)S(1)}, u32[]{:S(2)}, u32[]{:S(2)}) collective-permute-start(f32[4,64,128]{2,1,0:T(8,128)S(1)} %get-tuple-element.1155), channel_id=1, source_target_pairs={{0,8},{1,9},{2,10},{3,11},{4,12},{5,13},{6,14},{7,15},{16,24},{17,... | collective-permute-start | bytes 393224 | tf_op jit(solution)/shard_map/while/body/eval_jaxpr/ppermute | solution.py:12
  178.4 6.3 %collective-permute-start = (f32[4,64,128]{2,1,0:T(8,128)S(1)}, f32[4,64,128]{2,1,0:T(8,128)S(1)}, u32[]{:S(2)}, u32[]{:S(2)}) collective-permute-start(f32[4,64,128]{2,1,0:T(8,128)S(1)} %dynamic-slice_select_fusion.2), channel_id=1, source_target_pairs={{0,1},{1,2},{2,3},{3,4},{4,5},{5,6},{6,7},{7,0},{8,9},{9,10},{10,1... | collective-permute-start | bytes 393224 | tf_op jit(solution)/shard_map/while/body/eval_jaxpr/ppermute | solution.py:51
  184.8 6.3 %collective-permute-start.2 = (f32[4,64,128]{2,1,0:T(8,128)S(1)}, f32[4,64,128]{2,1,0:T(8,128)S(1)}, u32[]{:S(2)}, u32[]{:S(2)}) collective-permute-start(f32[4,64,128]{2,1,0:T(8,128)S(1)} %collective-permute-done), channel_id=1, source_target_pairs={{0,1},{1,2},{2,3},{3,4},{4,5},{5,6},{6,7},{7,0},{8,9},{9,10},{10,1... | collective-permute-start | bytes 393224 | tf_op jit(solution)/shard_map/while/body/eval_jaxpr/ppermute | solution.py:51
  184.8 6.3 %collective-permute-start.3 = (f32[4,64,128]{2,1,0:T(8,128)S(1)}, f32[4,64,128]{2,1,0:T(8,128)S(1)}, u32[]{:S(2)}, u32[]{:S(2)}) collective-permute-start(f32[4,64,128]{2,1,0:T(8,128)S(1)} %collective-permute-done.1), channel_id=1, source_target_pairs={{0,7},{1,0},{2,1},{3,2},{4,3},{5,4},{6,5},{7,6},{8,15},{9,8},{10,9... | collective-permute-start | bytes 393224 | tf_op jit(solution)/shard_map/while/body/eval_jaxpr/ppermute | solution.py:56
  203.5 15.8 %collective-permute-start.7 = (f32[4,64,128]{2,1,0:T(8,128)S(1)}, f32[4,64,128]{2,1,0:T(8,128)S(1)}, u32[]{:S(2)}, u32[]{:S(2)}) collective-permute-start(f32[4,64,128]{2,1,0:T(8,128)S(1)} %get-tuple-element.1155), channel_id=1, source_target_pairs={{0,8},{1,9},{2,10},{3,11},{4,12},{5,13},{6,14},{7,15},{16,24},{17,... | collective-permute-start | bytes 393224 | tf_op jit(solution)/shard_map/while/body/eval_jaxpr/ppermute | solution.py:12
  (18 other events, 109.4 us)
